TPU v7x, 512 devices: a whole 4x8x8 slice. The times are simulated.
512 devices in a mesh: seq: 128 (over y, z, core), tp: 4 (over x).
Axes of the slice: x: 4, y: 8, z: 8, core: 2. Of those that a mesh axis runs over, the one named last changes fastest.
Arguments:
- queries: bfloat16 [16384, 4096], P('seq', 'tp'), may hold values from -12 to 12
- keys: bfloat16 [16384, 512], P('seq', 'tp'), may hold values from -12 to 12
- values: bfloat16 [16384, 512], P('seq', 'tp'), may hold values from -6 to 6
- sinks: float32 [64], P('tp'), may hold values from 0.5 to 4.5
- session_start: int32 [16384], P('seq'), may hold values from 0 to 16383, as said below
- residual: bfloat16 [16384, 2880], P('seq', 'tp'), may hold values from -40 to 40
- w_out: bfloat16 [4096, 2880], P('seq', 'tp'), may hold values from -0.09375 to 0.09375
- norm_gain: float32 [2880], P('tp'), may hold values from 0.1 to 1.9
- expert_ids: int32 [16384, 4], P('seq'), may hold values from 0 to 63, all different within a row; in each aligned block of 128 rows (0 to 127, 128 to 255, ...) at most 10 rows name the same one
- expert_gates: bfloat16 [16384, 4], P('seq'), may hold values from 0.099609375 to 0.59765625
- w_gate: bfloat16 [2880, 92160], P('tp', 'seq'), may hold values from -0.109375 to 0.109375
- w_up: bfloat16 [2880, 92160], P('tp', 'seq'), may hold values from -0.109375 to 0.109375
- w_down: bfloat16 [92160, 2880], P('seq', 'tp'), may hold values from -0.15625 to 0.15625
Outputs:
- layer_out: bfloat16 [16384, 2880], P('seq', 'tp')
Inputs may be any that keep to these rules, and one draw needn't show every extreme that they name: `expert_ids`: each row names 4 different experts. Within the rows of one seq index (aligned blocks of 128 rows) no expert is named by more than 10 rows, a bound that some block reaches. `session_start`: nondecreasing; each entry is the first position of its token's session, so session_start[i] <= i, with equality at a session's first token.
All inputs are finite; a program needn't handle non-finite values.
Results may differ from a plain program's by a relative error of at most 0.013.
Values may be sent and summed in bfloat16 or wider, within the bound.
No kernel may reach another device: no remote copies, remote signals or barrier semaphores. Data moves between devices by JAX's collectives and lax.ppermute only.
A program may use at most 64 MiB of HBM per device.

v0:
```python
import jax
import jax.numpy as jnp
from jax import lax
from jax.sharding import PartitionSpec as P

D = 2880
HEAD_SIZE = 64
WINDOW_SPAN = 128
TOP = 4
NEGATIVE = -1e30
EPSILON = 1e-05


def passed_along(block, axis, distance):
    devices = range(lax.axis_size(axis))
    route = [(i - distance, i) for i in devices if i - distance in devices]
    return lax.ppermute(block, axis, route)


def shards(
    queries,
    keys,
    values,
    sinks,
    session_start,
    residual,
    w_out,
    norm_gain,
    expert_ids,
    expert_gates,
    w_gate,
    w_up,
    w_down,
):
    tok_count = queries.shape[0]
    kv_heads = keys.shape[1] // HEAD_SIZE
    q_heads = queries.shape[1] // HEAD_SIZE
    query_groups = q_heads // kv_heads
    seq_index = lax.axis_index("seq")
    first_pos = seq_index * tok_count
    tail_rows = passed_along((keys, values), "seq", 1)
    all_keys = jnp.concatenate([tail_rows[0], keys], axis=0)
    all_values = jnp.concatenate([tail_rows[1], values], axis=0)
    key_count = all_keys.shape[0]
    query_pos = first_pos + jnp.arange(tok_count, dtype=jnp.int32)
    key_pos = first_pos - WINDOW_SPAN + jnp.arange(key_count, dtype=jnp.int32)
    distance = query_pos[:, None] - key_pos[None, :]
    allowed = (
        (distance >= 0) & (distance < WINDOW_SPAN) & (key_pos[None, :] >= session_start[:, None])
    )
    blocked_queries = queries.reshape(tok_count, kv_heads, query_groups, HEAD_SIZE)
    blocked_keys = all_keys.reshape(key_count, kv_heads, HEAD_SIZE)
    blocked_values = all_values.reshape(key_count, kv_heads, HEAD_SIZE)
    scores = jnp.einsum(
        "qhgd,khd->hgqk", blocked_queries, blocked_keys, preferred_element_type=jnp.float32
    ) * HEAD_SIZE ** (-0.5)
    scores = jnp.where(allowed[None, None], scores, NEGATIVE)
    sink_column = sinks.reshape(kv_heads, query_groups)[:, :, None, None]
    row_max = jnp.maximum(jnp.max(scores, axis=-1, keepdims=True), sink_column)
    numerator = jnp.exp(scores - row_max) * allowed[None, None].astype(jnp.float32)
    denominator = jnp.sum(numerator, axis=-1, keepdims=True) + jnp.exp(sink_column - row_max)
    weights = (numerator / denominator).astype(jnp.bfloat16)
    head_out = jnp.einsum(
        "hgqk,khd->qhgd", weights, blocked_values, preferred_element_type=jnp.float32
    )
    head_out = head_out.astype(jnp.bfloat16).reshape(tok_count, q_heads * HEAD_SIZE)
    gathered = lax.all_gather(head_out, "tp", axis=1, tiled=True)
    attended = jnp.dot(
        gathered,
        lax.all_gather(w_out, "seq", axis=0, tiled=True),
        preferred_element_type=jnp.float32,
    )
    stream = residual.astype(jnp.float32) + attended
    squares = lax.psum(jnp.sum(stream * stream, axis=1), "tp")
    normed = (stream * lax.rsqrt(squares / D + EPSILON)[:, None] * norm_gain[None, :]).astype(
        jnp.bfloat16
    )
    seq_count = lax.axis_size("seq")
    experts = seq_count // 2
    capacity = 2 * ((5 * tok_count * TOP + 8 * experts - 1) // (8 * experts))
    present = expert_ids[:, :, None] == jnp.arange(experts, dtype=jnp.int32)[None, None, :]
    per_row = jnp.sum(present.astype(jnp.int32), axis=1)
    before = jnp.cumsum(per_row, axis=0) - per_row
    position = jnp.sum(jnp.where(present, before[:, None, :], 0), axis=2)
    halves = jnp.arange(2, dtype=jnp.int32)
    targets = (2 * expert_ids[:, :, None] + halves[None, None, :]) * capacity + position[:, :, None]
    slot_count = seq_count * capacity
    slot_ids = jnp.arange(slot_count, dtype=jnp.int32)
    quarter = normed.shape[1]
    matches = (slot_ids[:, None, None, None] == targets[None]).astype(jnp.bfloat16)
    routing = jnp.sum(matches, axis=(2, 3))
    sending = jnp.dot(routing, normed, preferred_element_type=jnp.float32).astype(jnp.bfloat16)
    arrived = lax.all_to_all(
        sending.reshape(seq_count, capacity, quarter),
        "seq",
        split_axis=0,
        concat_axis=0,
        tiled=True,
    )
    expert_rows = arrived.reshape(slot_count, quarter)
    gate_part = jnp.dot(expert_rows, w_gate, preferred_element_type=jnp.float32)
    up_part = jnp.dot(expert_rows, w_up, preferred_element_type=jnp.float32)
    gate_sum, up_sum = (
        lax.psum_scatter(
            gate_part.astype(jnp.bfloat16), "tp", scatter_dimension=1, tiled=True
        ).astype(jnp.float32),
        lax.psum_scatter(
            up_part.astype(jnp.bfloat16), "tp", scatter_dimension=1, tiled=True
        ).astype(jnp.float32),
    )
    active = (jax.nn.silu(gate_sum) * up_sum).astype(jnp.bfloat16)
    produced = jnp.dot(
        lax.all_gather(active, "tp", axis=1, tiled=True), w_down, preferred_element_type=jnp.float32
    )
    produced = produced.astype(jnp.bfloat16).reshape(seq_count, capacity, quarter)
    returned = lax.all_to_all(produced, "seq", split_axis=0, concat_axis=0, tiled=True)
    both = returned.reshape(experts, 2, capacity, quarter)
    paired = (both[:, 0].astype(jnp.float32) + both[:, 1].astype(jnp.float32)).astype(jnp.bfloat16)
    paired = paired.reshape(experts * capacity, quarter)
    pair_slot = expert_ids * capacity + position
    pair_ids = jnp.arange(experts * capacity, dtype=jnp.int32)
    mixing = jnp.where(
        pair_ids[None, :, None] == pair_slot[:, None, :],
        expert_gates[:, None, :],
        jnp.zeros((), jnp.bfloat16),
    )
    mixing = jnp.sum(mixing, axis=2)
    blended = jnp.dot(mixing, paired, preferred_element_type=jnp.float32)
    return (stream + blended).astype(jnp.bfloat16)


def solution(mesh):
    return jax.shard_map(
        shards,
        mesh=mesh,
        in_specs=(
            P("seq", "tp"),
            P("seq", "tp"),
            P("seq", "tp"),
            P("tp"),
            P("seq"),
            P("seq", "tp"),
            P("seq", "tp"),
            P("tp"),
            P("seq", None),
            P("seq", None),
            P("tp", "seq"),
            P("tp", "seq"),
            P("seq", "tp"),
        ),
        out_specs=P("seq", "tp"),
        check_vma=False,
    )
```

profile of v0, /device:TPU:72, one launch (start us, length us, event | category | flops | bytes accessed | tf_op | source)
XLA Modules:
  0.0 459.0 jit_solution(16349413189414434142)
XLA Ops:
  6.5 2.0 collective-permute-start.1
  8.6 4.4 collective-permute-start
  13.0 1.4 fusion.18
  14.4 1.1 copy.51
  17.8 1.4 fusion.4
  20.1 1.4 convolution_convert_fusion.4
  23.4 30.5 %all-gather.5.cloned.1.call-done = bf16[128,4096]{0,1:T(8,128)(2,1)} async-done(((bf16[128,1024]{0,1:T(8,128)(2,1)}), bf16[128,4096]{0,1:T(8,128)(2,1)}) %all-gather.5.cloned.1.call-update) | async-done | bytes 1048592 | tf_op jit(solution)/shard_map/all_gather | solution.py:67
  53.9 88.6 %all-gather.7.cloned.1.call-done = bf16[4096,720]{1,0:T(8,128)(2,1)} async-done(((bf16[32,720]{1,0:T(8,128)(2,1)}), bf16[4096,720]{1,0:T(8,128)(2,1)}) %all-gather.7.cloned.1.call-update) | async-done | bytes 5898256 | tf_op jit(solution)/shard_map/all_gather | solution.py:70
  142.5 5.1 %multiply_reduce_fusion = (f32[128]{0:T(128)S(1)}, f32[128,720]{0,1:T(8,128)S(1)}) fusion(bf16[128,4096]{0,1:T(8,128)(2,1)} %all-gather.5.cloned.1.call-done, bf16[4096,720]{1,0:T(8,128)(2,1)} %all-gather.7.cloned.1.call-done, bf16[128,720]{0,1:T(8,128)(2,1)} %param.18), kind=kOutput, calls=%fused_computation.31 | convolution fusion | flops 755343232 | bytes 7500288 | tf_op jit(solution)/shard_map/dot_general | solution.py:68
  147.6 10.4 %psum.7 = f32[128]{0:T(128)S(1)} all-reduce(f32[128]{0:T(128)S(1)} %get-tuple-element.15), channel_id=1, replica_groups=mesh['seq'=128,'tp'=4] {'tp'}, use_global_device_ids=true, to_apply=%region_8.9 | all-reduce | flops 128 | bytes 1024 | tf_op jit(solution)/shard_map/psum | solution.py:74
  158.0 2.0 convolution_convert_fusion
  160.0 2.6 copy.56
  162.6 2.5 reshape.190
  165.1 86.3 %all_to_all.10 = bf16[128,10,720]{2,1,0:T(8,128)(2,1)} all-to-all(bf16[128,10,720]{2,1,0:T(8,128)(2,1)} %reshape.190), channel_id=1, replica_groups=mesh['seq'=128,'tp'=4] {'seq'}, dimensions={0} | all-to-all | bytes 3686400 | tf_op jit(solution)/shard_map/all_to_all | solution.py:93
  251.4 3.9 reshape.191
  255.4 3.0 convolution_convert_fusion.2
  258.4 2.9 convolution_convert_fusion.3
  261.3 46.3 %fusion.22 = (bf16[1280,184]{0,1:T(8,128)(2,1)S(1)}, bf16[1280,184]{0,1:T(8,128)(2,1)S(1)}) fusion(bf16[1280,720]{0,1:T(8,128)(2,1)} %convolution_convert_fusion.2, bf16[1280,720]{0,1:T(8,128)(2,1)} %convolution_convert_fusion.3), kind=kCustom, calls=%all-reduce-scatter.2 | all-reduce-scatter fusion | flops 1884161 | bytes 4630528
  307.7 1.3 collective-permute-start.2
  309.0 3.3 collective-permute-start.3
  312.3 1.3 dynamic-slice.6
  315.6 1.2 fusion.14
  316.8 29.1 %all-gather.9.cloned.1.call-done = bf16[4,180,1280]{2,1,0:T(8,128)(2,1)} async-done(((bf16[1,180,1280]{2,1,0:T(8,128)(2,1)}), bf16[4,180,1280]{2,1,0:T(8,128)(2,1)}) %all-gather.9.cloned.1.call-update) | async-done | bytes 1843216 | tf_op jit(solution)/shard_map/all_gather | solution.py:113
  345.9 1.7 reshape.195
  347.5 4.2 convolution_convert_fusion.1
  351.8 2.6 copy.57
  354.4 2.5 reshape.192
  356.9 14.5 %all-to-all-start.1 = ((bf16[128,10,720]{2,1,0:T(8,128)(2,1)}), bf16[128,10,720]{2,1,0:T(8,128)(2,1)}, u32[]{:S(2)}, u32[]{:S(2)}) async-start(bf16[128,10,720]{2,1,0:T(8,128)(2,1)} %reshape.192), calls=%async_computation.1 | async-start | bytes 6291456 | tf_op jit(solution)/shard_map/all_to_all | solution.py:116
  371.7 74.7 %all-to-all-done.1 = bf16[128,10,720]{2,1,0:T(8,128)(2,1)} async-done(((bf16[128,10,720]{2,1,0:T(8,128)(2,1)}), bf16[128,10,720]{2,1,0:T(8,128)(2,1)}, u32[]{:S(2)}, u32[]{:S(2)}) %all-to-all-start.1) | async-done | bytes 1843232 | tf_op jit(solution)/shard_map/all_to_all | solution.py:116
  446.4 2.3 add_convert_fusion
  448.7 1.4 convert_element_type.92
  450.1 2.4 fusion.7
  (51 shorter events, 6.5 us)
Async XLA Ops:
  6.5 248.8 %copy-start = (bf16[720,720]{1,0:T(8,128)(2,1)S(1)}, bf16[720,720]{1,0:T(8,128)(2,1)}, u32[]{:S(2)}) copy-start(bf16[720,720]{1,0:T(8,128)(2,1)} %param.24) | copy-start | bytes 3110404
  6.5 47.4 %all-gather.5.cloned.1.call-start = ((), (), s32[]{:S(2)}) async-start(), calls=%async_computation.2 | async-start | bytes 1310720 | tf_op jit(solution)/shard_map/all_gather | solution.py:67
  6.5 9.8 %collective-permute-start.1 = (bf16[128,128]{1,0:T(8,128)(2,1)}, bf16[128,128]{1,0:T(8,128)(2,1)S(1)}, u32[]{:S(2)}, u32[]{:S(2)}) collective-permute-start(bf16[128,128]{1,0:T(8,128)(2,1)} %param.14), channel_id=1, source_target_pairs={{0,4},{4,8},{8,12},{12,16},{16,20},{20,24},{24,28},{28,32},{32,36}... | collective-permute-start | bytes 98312 | tf_op jit(solution)/shard_map/ppermute | solution.py:17
  8.6 11.3 %collective-permute-start = (bf16[128,128]{1,0:T(8,128)(2,1)}, bf16[128,128]{1,0:T(8,128)(2,1)S(1)}, u32[]{:S(2)}, u32[]{:S(2)}) collective-permute-start(bf16[128,128]{1,0:T(8,128)(2,1)} %param.15), channel_id=1, source_target_pairs={{0,4},{4,8},{8,12},{12,16},{16,20},{20,24},{24,28},{28,32},{32,36}... | collective-permute-start | bytes 98312 | tf_op jit(solution)/shard_map/ppermute | solution.py:17
  17.8 1.5 copy-start.1
  17.8 2.0 copy-start.3
  19.2 0.9 copy-start.2
  20.1 2.2 copy-start.4
  21.5 121.0 %all-gather.7.cloned.1.call-start = ((), (), s32[]{:S(2)}) async-start(), calls=%async_computation.3 | async-start | bytes 6340608 | tf_op jit(solution)/shard_map/all_gather | solution.py:70
  22.3 323.6 %all-gather.9.cloned.1.call-start = ((), (), s32[]{:S(2)}) async-start(), calls=%async_computation.4 | async-start | bytes 2355200 | tf_op jit(solution)/shard_map/all_gather | solution.py:113
  23.4 134.6 %copy-start.5 = (f32[720]{0:T(1024)S(1)}, f32[720]{0:T(1024)}, u32[]{:S(2)}) copy-start(f32[720]{0:T(1024)} %param.20) | copy-start | bytes 8644
  255.4 3.0 copy-start.7
  307.7 6.6 %collective-permute-start.2 = (bf16[1280,12]{0,1:T(8,128)(2,1)S(1)}, bf16[1280,12]{0,1:T(8,128)(2,1)S(1)}, u32[]{:S(2)}, u32[]{:S(2)}) collective-permute-start(bf16[1280,12]{0,1:T(8,128)(2,1)S(1)} %slice.10), channel_id=1, source_target_pairs={{0,1},{1,2},{2,3},{4,5},{5,6},{6,7},{8,9},{9,10},{10,11},{12,13},{... | collective-permute-start | bytes 92168
  309.0 5.9 %collective-permute-start.3 = (bf16[1280,12]{0,1:T(8,128)(2,1)S(1)}, bf16[1280,12]{0,1:T(8,128)(2,1)S(1)}, u32[]{:S(2)}, u32[]{:S(2)}) collective-permute-start(bf16[1280,12]{0,1:T(8,128)(2,1)S(1)} %slice.11), channel_id=1, source_target_pairs={{0,1},{1,2},{2,3},{4,5},{5,6},{6,7},{8,9},{9,10},{10,11},{12,13},{... | collective-permute-start | bytes 92168
  356.9 14.5 %copy-start.6 = (bf16[128,4]{0,1:T(4,128)(2,1)S(1)}, bf16[128,4]{0,1:T(4,128)(2,1)}, u32[]{:S(2)}) copy-start(bf16[128,4]{0,1:T(4,128)(2,1)} %param.22) | copy-start | bytes 3076
  356.9 89.5 %all-to-all-start.1 = ((bf16[128,10,720]{2,1,0:T(8,128)(2,1)}), bf16[128,10,720]{2,1,0:T(8,128)(2,1)}, u32[]{:S(2)}, u32[]{:S(2)}) async-start(bf16[128,10,720]{2,1,0:T(8,128)(2,1)} %reshape.192), calls=%async_computation.1 | async-start | bytes 6291456 | tf_op jit(solution)/shard_map/all_to_all | solution.py:116
Sparse Core Ops, SparseCore 0:
  21.6 32.2 all-gather.4
  57.0 85.4 all-gather.6
  316.9 28.9 all-gather.8
where the time goes:
time: 460 us; the launch traced here: 459 us
  waiting for transfers between devices  224 us (49%)
  blocking collectives  143 us (31%)
  starting transfers between devices  25.6 us (6%)
  local copies, waits for them, and re-layouts  22.8 us (5%)
  matrix products  22.4 us (5%)
  between operations  14.1 us (3%)
  other arithmetic  7.47 us (2%)
    all_gather x1, waiting for transfers between devices, shards(): lax.all_gather(w_out, 'seq', axis=0, tiled=True)  88.6 us
    all_to_all x1, blocking collectives, shards(): lax.all_to_all(sending.reshape(seq_count, capacity, quarter), 'seq', spli...  86.3 us
    all_to_all x1, waiting for transfers between devices, shards(): lax.all_to_all(produced, 'seq', split_axis=0, concat_axis=0, tiled=True)  74.7 us
    unnamed x1, blocking collectives  46.3 us
    all_gather x1, waiting for transfers between devices, shards(): gathered = lax.all_gather(head_out, 'tp', axis=1, tiled=True)  30.5 us
    all_gather x1, waiting for transfers between devices, shards(): lax.all_gather(active, 'tp', axis=1, tiled=True)  29.1 us
    all_to_all x1, starting transfers between devices, shards(): lax.all_to_all(produced, 'seq', split_axis=0, concat_axis=0, tiled=True)  14.5 us
    psum x1, blocking collectives, shards(): squares = lax.psum(jnp.sum(stream * stream, axis=1), 'tp')  10.4 us
  transfers between devices with their start and end apart: 8, of which 4 were waited for; matrix products, arithmetic and copies ran while one was open for 2% of the time, Pallas kernels for 0%

commit v1 on v0

--- a/solution.py
+++ b/solution.py
@@ -2,6 +2,7 @@
 import jax.numpy as jnp
 from jax import lax
 from jax.sharding import PartitionSpec as P
+from jax.lax import all_to_all, axis_size
 
 D = 2880
 HEAD_SIZE = 64
@@ -64,7 +65,10 @@
         "hgqk,khd->qhgd", weights, blocked_values, preferred_element_type=jnp.float32
     )
     head_out = head_out.astype(jnp.bfloat16).reshape(tok_count, q_heads * HEAD_SIZE)
-    gathered = lax.all_gather(head_out, "tp", axis=1, tiled=True)
+    gathered = jnp.concatenate(
+        all_to_all(jnp.stack([head_out for _ in range(axis_size("tp"))], axis=0), "tp", 0, 0),
+        axis=1,
+    )
     attended = jnp.dot(
         gathered,
         lax.all_gather(w_out, "seq", axis=0, tiled=True),

time: 460 us -> 417 us (0.907)
  waiting for transfers between devices: 224 us -> 177 us
    all_gather x1 -> x0, waiting for transfers between devices: 30.5 us -> none  [shards(): gathered = lax.all_gather(head_out, 'tp', axis=1, tiled=True)]
    all_gather x1, waiting for transfers between devices: 88.6 us -> 58.8 us  [shards(): lax.all_gather(w_out, 'seq', axis=0, tiled=True)]
    all_to_all x0 -> x1, waiting for transfers between devices: none -> 14.2 us  [shards(): all_to_all(jnp.stack([head_out for _ in range(axis_size('tp'))], axis=0),...]
  transfers between devices with their start and end apart: 8 -> 8, of which waited for: 4 -> 4; matrix products, arithmetic and copies ran while one was open for 2% -> 3% of each run, Pallas kernels for 0% -> 0%
where the time goes in v1:
time: 417 us; the launch traced here: 416 us
  waiting for transfers between devices  177 us (42%)
  blocking collectives  143 us (34%)
  starting transfers between devices  29.7 us (7%)
  local copies, waits for them, and re-layouts  23.2 us (6%)
  matrix products  20.6 us (5%)
  between operations  14.3 us (3%)
  other arithmetic  7.58 us (2%)
    all_to_all x1, blocking collectives, shards(): lax.all_to_all(sending.reshape(seq_count, capacity, quarter), 'seq', spli...  86.3 us
    all_to_all x1, waiting for transfers between devices, shards(): lax.all_to_all(produced, 'seq', split_axis=0, concat_axis=0, tiled=True)  74.7 us
    all_gather x1, waiting for transfers between devices, shards(): lax.all_gather(w_out, 'seq', axis=0, tiled=True)  58.8 us
    unnamed x1, blocking collectives  46.3 us
    all_gather x1, waiting for transfers between devices, shards(): lax.all_gather(active, 'tp', axis=1, tiled=True)  29.1 us
    all_to_all x1, starting transfers between devices, shards(): lax.all_to_all(produced, 'seq', split_axis=0, concat_axis=0, tiled=True)  14.5 us
    all_to_all x1, waiting for transfers between devices, shards(): all_to_all(jnp.stack([head_out for _ in range(axis_size('tp'))], axis=0),...  14.2 us
    psum x1, blocking collectives, shards(): squares = lax.psum(jnp.sum(stream * stream, axis=1), 'tp')  10.4 us
  transfers between devices with their start and end apart: 8, of which 4 were waited for; matrix products, arithmetic and copies ran while one was open for 3% of the time, Pallas kernels for 0%

profile of v1, /device:TPU:72, one launch (start us, length us, event | category | flops | bytes accessed | tf_op | source)
XLA Modules:
  0.0 416.0 jit_solution(3368298067839414780)
XLA Ops:
  7.3 1.9 collective-permute-start.1
  9.2 4.4 %collective-permute-start = (bf16[128,128]{1,0:T(8,128)(2,1)}, bf16[128,128]{1,0:T(8,128)(2,1)S(1)}, u32[]{:S(2)}, u32[]{:S(2)}) collective-permute-start(bf16[128,128]{1,0:T(8,128)(2,1)} %param.15), channel_id=1, source_target_pairs={{0,4},{4,8},{8,12},{12,16},{16,20},{20,24},{24,28},{28,32},{32,36}... | collective-permute-start | bytes 98312 | tf_op jit(solution)/shard_map/ppermute | solution.py:18
  13.6 0.8 fusion.18
  14.4 1.1 copy.52
  19.9 1.1 stack.3
  21.1 4.3 %all-to-all-start = ((bf16[4,128,1024]{1,2,0:T(8,128)(2,1)}), bf16[4,128,1024]{1,2,0:T(8,128)(2,1)S(1)}, u32[]{:S(2)}, u32[]{:S(2)}) async-start(bf16[4,128,1024]{1,2,0:T(8,128)(2,1)} %stack.3), calls=%async_computation | async-start | bytes 2097152 | tf_op jit(solution)/shard_map/all_to_all | solution.py:69
  26.5 14.2 %all-to-all-done = bf16[4,128,1024]{1,2,0:T(8,128)(2,1)S(1)} async-done(((bf16[4,128,1024]{1,2,0:T(8,128)(2,1)}), bf16[4,128,1024]{1,2,0:T(8,128)(2,1)S(1)}, u32[]{:S(2)}, u32[]{:S(2)}) %all-to-all-start) | async-done | bytes 1048608 | tf_op jit(solution)/shard_map/all_to_all | solution.py:69
  40.6 58.8 %all-gather.4.cloned.1.call-done = bf16[4096,720]{1,0:T(8,128)(2,1)} async-done(((bf16[32,720]{1,0:T(8,128)(2,1)}), bf16[4096,720]{1,0:T(8,128)(2,1)}) %all-gather.4.cloned.1.call-update) | async-done | bytes 5898256 | tf_op jit(solution)/shard_map/all_gather | solution.py:74
  99.4 4.9 %multiply_reduce_fusion = (f32[128]{0:T(128)S(1)}, f32[128,720]{0,1:T(8,128)S(1)}) fusion(bf16[128,4096]{0,1:T(8,128)(2,1)S(1)} %bitcast.63, bf16[4096,720]{1,0:T(8,128)(2,1)} %all-gather.4.cloned.1.call-done, bf16[128,720]{0,1:T(8,128)(2,1)S(1)} %copy-done.1), kind=kOutput, calls=%fused_computation.31 | convolution fusion | flops 755343232 | bytes 7500288 | tf_op jit(solution)/shard_map/dot_general | solution.py:72
  104.3 10.4 %psum.7 = f32[128]{0:T(128)S(1)} all-reduce(f32[128]{0:T(128)S(1)} %get-tuple-element.15), channel_id=1, replica_groups=mesh['seq'=128,'tp'=4] {'tp'}, use_global_device_ids=true, to_apply=%region_8.9 | all-reduce | flops 128 | bytes 1024 | tf_op jit(solution)/shard_map/psum | solution.py:78
  114.7 2.0 convolution_convert_fusion
  116.7 2.6 copy.57
  119.3 2.5 reshape.196
  121.8 86.3 %all_to_all.15 = bf16[128,10,720]{2,1,0:T(8,128)(2,1)} all-to-all(bf16[128,10,720]{2,1,0:T(8,128)(2,1)} %reshape.196), channel_id=1, replica_groups=mesh['seq'=128,'tp'=4] {'seq'}, dimensions={0} | all-to-all | bytes 3686400 | tf_op jit(solution)/shard_map/all_to_all | solution.py:97
  208.1 3.9 reshape.197
  212.1 3.0 convolution_convert_fusion.2
  215.1 2.9 convolution_convert_fusion.3
  218.0 46.3 %fusion.22 = (bf16[1280,184]{0,1:T(8,128)(2,1)S(1)}, bf16[1280,184]{0,1:T(8,128)(2,1)S(1)}) fusion(bf16[1280,720]{0,1:T(8,128)(2,1)} %convolution_convert_fusion.2, bf16[1280,720]{0,1:T(8,128)(2,1)} %convolution_convert_fusion.3), kind=kCustom, calls=%all-reduce-scatter.2 | all-reduce-scatter fusion | flops 1884161 | bytes 4630528
  264.4 1.3 collective-permute-start.2
  265.7 3.3 collective-permute-start.3
  269.0 1.3 dynamic-slice.6
  272.3 1.2 fusion.14
  273.5 29.1 %all-gather.6.cloned.1.call-done = bf16[4,180,1280]{2,1,0:T(8,128)(2,1)} async-done(((bf16[1,180,1280]{2,1,0:T(8,128)(2,1)}), bf16[4,180,1280]{2,1,0:T(8,128)(2,1)}) %all-gather.6.cloned.1.call-update) | async-done | bytes 1843216 | tf_op jit(solution)/shard_map/all_gather | solution.py:117
  302.6 1.7 reshape.201
  304.2 4.2 %convolution_convert_fusion.1 = bf16[1280,720]{0,1:T(8,128)(2,1)} fusion(bf16[720,1280]{1,0:T(8,128)(2,1)S(1)} %reshape.201, bf16[720,720]{1,0:T(8,128)(2,1)} %param.25), kind=kOutput, calls=%fused_computation.3 | convolution fusion | flops 1328025600 | bytes 4723200 | tf_op jit(solution)/shard_map/dot_general | solution.py:116
  308.5 2.6 copy.58
  311.1 2.5 reshape.198
  313.6 14.5 %all-to-all-start.2 = ((bf16[128,10,720]{2,1,0:T(8,128)(2,1)}), bf16[128,10,720]{2,1,0:T(8,128)(2,1)}, u32[]{:S(2)}, u32[]{:S(2)}) async-start(bf16[128,10,720]{2,1,0:T(8,128)(2,1)} %reshape.198), calls=%async_computation.2 | async-start | bytes 6291456 | tf_op jit(solution)/shard_map/all_to_all | solution.py:120
  328.4 74.7 %all-to-all-done.2 = bf16[128,10,720]{2,1,0:T(8,128)(2,1)} async-done(((bf16[128,10,720]{2,1,0:T(8,128)(2,1)}), bf16[128,10,720]{2,1,0:T(8,128)(2,1)}, u32[]{:S(2)}, u32[]{:S(2)}) %all-to-all-start.2) | async-done | bytes 1843232 | tf_op jit(solution)/shard_map/all_to_all | solution.py:120
  403.1 2.3 add_convert_fusion
  405.4 1.4 convert_element_type.92
  406.8 2.4 fusion.7
  (47 shorter events, 7.7 us)
Async XLA Ops:
  6.5 205.5 %copy-start = (bf16[720,720]{1,0:T(8,128)(2,1)S(1)}, bf16[720,720]{1,0:T(8,128)(2,1)}, u32[]{:S(2)}) copy-start(bf16[720,720]{1,0:T(8,128)(2,1)} %param.24) | copy-start | bytes 3110404
  6.5 92.9 %all-gather.4.cloned.1.call-start = ((), (), s32[]{:S(2)}) async-start(), calls=%async_computation.3 | async-start | bytes 6340608 | tf_op jit(solution)/shard_map/all_gather | solution.py:74
  7.3 9.0 %collective-permute-start.1 = (bf16[128,128]{1,0:T(8,128)(2,1)}, bf16[128,128]{1,0:T(8,128)(2,1)S(1)}, u32[]{:S(2)}, u32[]{:S(2)}) collective-permute-start(bf16[128,128]{1,0:T(8,128)(2,1)} %param.14), channel_id=1, source_target_pairs={{0,4},{4,8},{8,12},{12,16},{16,20},{20,24},{24,28},{28,32},{32,36}... | collective-permute-start | bytes 98312 | tf_op jit(solution)/shard_map/ppermute | solution.py:18
  9.2 7.9 %collective-permute-start = (bf16[128,128]{1,0:T(8,128)(2,1)}, bf16[128,128]{1,0:T(8,128)(2,1)S(1)}, u32[]{:S(2)}, u32[]{:S(2)}) collective-permute-start(bf16[128,128]{1,0:T(8,128)(2,1)} %param.15), channel_id=1, source_target_pairs={{0,4},{4,8},{8,12},{12,16},{16,20},{20,24},{24,28},{28,32},{32,36}... | collective-permute-start | bytes 98312 | tf_op jit(solution)/shard_map/ppermute | solution.py:18
  19.9 5.5 %copy-start.2 = (s32[128,4]{0,1:T(4,128)S(1)}, s32[128,4]{0,1:T(4,128)}, u32[]{:S(2)}) copy-start(s32[128,4]{0,1:T(4,128)} %param.21) | copy-start | bytes 6148
  19.9 79.5 %copy-start.1 = (bf16[128,720]{0,1:T(8,128)(2,1)S(1)}, bf16[128,720]{0,1:T(8,128)(2,1)}, u32[]{:S(2)}) copy-start(bf16[128,720]{0,1:T(8,128)(2,1)} %param.18) | copy-start | bytes 552964
  21.1 19.6 %all-to-all-start = ((bf16[4,128,1024]{1,2,0:T(8,128)(2,1)}), bf16[4,128,1024]{1,2,0:T(8,128)(2,1)S(1)}, u32[]{:S(2)}, u32[]{:S(2)}) async-start(bf16[4,128,1024]{1,2,0:T(8,128)(2,1)} %stack.3), calls=%async_computation | async-start | bytes 2097152 | tf_op jit(solution)/shard_map/all_to_all | solution.py:69
  25.4 277.2 %all-gather.6.cloned.1.call-start = ((), (), s32[]{:S(2)}) async-start(), calls=%async_computation.4 | async-start | bytes 2355200 | tf_op jit(solution)/shard_map/all_gather | solution.py:117
  99.4 15.3 %copy-start.3 = (f32[720]{0:T(1024)S(1)}, f32[720]{0:T(1024)}, u32[]{:S(2)}) copy-start(f32[720]{0:T(1024)} %param.20) | copy-start | bytes 8644
  212.1 3.0 copy-start.5
  264.4 6.6 %collective-permute-start.2 = (bf16[1280,12]{0,1:T(8,128)(2,1)S(1)}, bf16[1280,12]{0,1:T(8,128)(2,1)S(1)}, u32[]{:S(2)}, u32[]{:S(2)}) collective-permute-start(bf16[1280,12]{0,1:T(8,128)(2,1)S(1)} %slice.10), channel_id=1, source_target_pairs={{0,1},{1,2},{2,3},{4,5},{5,6},{6,7},{8,9},{9,10},{10,11},{12,13},{... | collective-permute-start | bytes 92168
  265.7 5.9 %collective-permute-start.3 = (bf16[1280,12]{0,1:T(8,128)(2,1)S(1)}, bf16[1280,12]{0,1:T(8,128)(2,1)S(1)}, u32[]{:S(2)}, u32[]{:S(2)}) collective-permute-start(bf16[1280,12]{0,1:T(8,128)(2,1)S(1)} %slice.11), channel_id=1, source_target_pairs={{0,1},{1,2},{2,3},{4,5},{5,6},{6,7},{8,9},{9,10},{10,11},{12,13},{... | collective-permute-start | bytes 92168
  313.6 14.5 %copy-start.4 = (bf16[128,4]{0,1:T(4,128)(2,1)S(1)}, bf16[128,4]{0,1:T(4,128)(2,1)}, u32[]{:S(2)}) copy-start(bf16[128,4]{0,1:T(4,128)(2,1)} %param.22) | copy-start | bytes 3076
  313.6 89.5 %all-to-all-start.2 = ((bf16[128,10,720]{2,1,0:T(8,128)(2,1)}), bf16[128,10,720]{2,1,0:T(8,128)(2,1)}, u32[]{:S(2)}, u32[]{:S(2)}) async-start(bf16[128,10,720]{2,1,0:T(8,128)(2,1)} %reshape.198), calls=%async_computation.2 | async-start | bytes 6291456 | tf_op jit(solution)/shard_map/all_to_all | solution.py:120
Sparse Core Ops, SparseCore 0:
  10.5 88.8 all-gather.3
  273.6 28.9 all-gather.5
